TPU v7x, 32 devices: a whole 2x2x4 slice. The times are simulated.
32 devices in a mesh: groups: 2 (over x), ctx: 16 (over z, y, core).
Axes of the slice: x: 2, y: 2, z: 4, core: 2. Of those that a mesh axis runs over, the one named last changes fastest.
Arguments:
- hidden_in: bfloat16 [4096, 2048], P(('groups', 'ctx')), parts along dimension 0, may hold values from -6 to 6
- queries: bfloat16 [4096, 1024], P(('groups', 'ctx')), parts along dimension 0, as said below
- keys: bfloat16 [4096, 128], P(('groups', 'ctx')), parts along dimension 0, as said below
- values: bfloat16 [4096, 128], P(('groups', 'ctx')), parts along dimension 0, may hold values from -6 to 6
- out_weight: bfloat16 [1024, 2048], replicated, may hold values from -0.5 to 0.5
- norm_gain: float32 [2048], replicated, may hold values from 0.1 to 1.9
- gate_weight: bfloat16 [2048, 11008], P(None, 'ctx'), may hold values from -0.125 to 0.125
- up_weight: bfloat16 [2048, 11008], P(None, 'ctx'), may hold values from -0.125 to 0.125
- down_weight: bfloat16 [11008, 2048], P('ctx'), may hold values from -0.0546875 to 0.0546875
- pair_ids: int32 [4096], P('groups'), parts along dimension 0, may hold values from 0 to 3, as said below
- roles: int32 [4096], P('groups'), parts along dimension 0, may hold values from 0 to 2, as said below
- send_rows: int32 [32, 128], P(('groups', 'ctx')), parts along dimension 0, may hold values from 0 to 127, as said below
- send_counts: int32 [32, 16], P('groups'), parts along dimension 0, may hold values from 0 to 8, as said below
Outputs:
- layer_out: bfloat16 [4096, 2048], P(('groups', 'ctx')), parts along dimension 0
There are 2 independent parts, one for each index of `groups`. A program takes and returns all parts, laid end to end along the dimension named above; an argument that names none is the same for every part. Nothing has to cross between parts.
Inputs may be any that keep to these rules, and one draw needn't show every extreme that they name: `pair_ids`: never falls along the sequence; every pair is present, and one pair's chosen response spans 256 positions or more. `roles`: each pair is a prompt, then its chosen response, then its rejected response, each of one position or more; responses fill exactly 1536 positions. `send_rows`: slots j * 8 + k with k < send_counts[i, j] list distinct local rows of device i, together exactly its positions whose role is not 0; other slots hold 0. `send_counts`: replicated on every device; every column sums to 96; some entry equals 8. `queries`: values within -8 to 8. `keys`: values within -8 to 8.
All inputs are finite; a program needn't handle non-finite values.
Results may differ from a plain program's by a relative error of at most 0.015.
Values may be sent and summed in bfloat16 or wider, within the bound.
A program may use at most 128 MiB of HBM per device.

v0:
```python
import jax
import jax.numpy as jnp
from jax import lax
from jax.sharding import PartitionSpec as P

NEG_FILL = -1e30


def on_device(
    hidden_in,
    queries,
    keys,
    values,
    out_weight,
    norm_gain,
    gate_weight,
    up_weight,
    down_weight,
    pair_ids,
    roles,
    send_rows,
    send_counts,
):
    devices = lax.axis_size("ctx")
    my_index = lax.axis_index("ctx")
    tok_rows = hidden_in.shape[0]
    head_dim = keys.shape[1]
    head_count = queries.shape[1] // head_dim
    own_begin = my_index * tok_rows
    query_pos = own_begin + jnp.arange(tok_rows, dtype=jnp.int32)
    query_pair = lax.dynamic_slice_in_dim(pair_ids, own_begin, tok_rows)
    query_role = lax.dynamic_slice_in_dim(roles, own_begin, tok_rows)
    query_heads = queries.reshape(tok_rows, head_count, head_dim)
    score_scale = 1.0 / head_dim**0.5
    key_piece = lax.all_gather(keys, "ctx", axis=0, tiled=True)
    value_piece = lax.all_gather(values, "ctx", axis=0, tiled=True)
    row_count = key_piece.shape[0]
    key_pos = jnp.arange(row_count, dtype=jnp.int32)
    seen_mask = (
        (query_pair[:, None] == pair_ids[None, :])
        & (key_pos[None, :] <= query_pos[:, None])
        & ((roles[None, :] == 0) | (roles[None, :] == query_role[:, None]))
    )
    maximum = jnp.full((head_count, tok_rows), NEG_FILL, jnp.float32)
    scores = (
        jnp.einsum("tqd,kd->qtk", query_heads, key_piece, preferred_element_type=jnp.float32)
        * score_scale
    )
    masked = jnp.where(seen_mask[None], scores, NEG_FILL)
    fresh_max = jnp.maximum(maximum, jnp.max(masked, axis=-1))
    weights = jnp.where(seen_mask[None], jnp.exp(masked - fresh_max[..., None]), 0.0)
    denominator = jnp.sum(weights, axis=-1)
    numerator = jnp.einsum(
        "qtk,kd->qtd", weights.astype(jnp.bfloat16), value_piece, preferred_element_type=jnp.float32
    )
    maximum, denominator, numerator = (fresh_max, denominator, numerator)
    attention = (
        (numerator / denominator[..., None])
        .transpose(1, 0, 2)
        .reshape(tok_rows, head_count * head_dim)
        .astype(jnp.bfloat16)
    )
    residual = (
        hidden_in.astype(jnp.float32)
        + jnp.dot(attention, out_weight, preferred_element_type=jnp.float32)
    ).astype(jnp.bfloat16)
    wide = residual.astype(jnp.float32)
    mean_sq = jnp.mean(wide * wide, axis=-1, keepdims=True)
    normed = (wide * lax.rsqrt(mean_sq + 1e-06) * norm_gain[None, :]).astype(jnp.bfloat16)
    slot_total = send_rows.shape[1]
    capacity = slot_total // devices
    rows_flat = send_rows[0]
    my_counts = lax.dynamic_slice_in_dim(send_counts, my_index, 1, 0)[0]
    valid = jnp.tile(jnp.arange(capacity, dtype=jnp.int32), devices) < jnp.repeat(
        my_counts, capacity
    )
    target = jnp.where(valid, rows_flat, tok_rows)
    gathered = lax.all_gather(normed, "ctx", axis=0, tiled=True)
    gate_out = jnp.dot(gathered, gate_weight, preferred_element_type=jnp.float32)
    up_out = jnp.dot(gathered, up_weight, preferred_element_type=jnp.float32)
    inner_out = (jax.nn.silu(gate_out) * up_out).astype(jnp.bfloat16)
    summed = lax.psum_scatter(
        jnp.dot(inner_out, down_weight, preferred_element_type=jnp.float32).astype(jnp.bfloat16),
        "ctx",
        scatter_dimension=0,
        tiled=True,
    )
    live_mask = jnp.zeros((tok_rows,), jnp.float32).at[target].set(1.0, mode="drop")
    ffn_round = lax.optimization_barrier(summed)
    ffn_back = ffn_round.astype(jnp.float32) * live_mask[:, None]
    return (residual.astype(jnp.float32) + ffn_back).astype(jnp.bfloat16)


def solution(mesh):
    return jax.shard_map(
        on_device,
        mesh=mesh,
        in_specs=(
            P(("groups", "ctx"), None),
            P(("groups", "ctx"), None),
            P(("groups", "ctx"), None),
            P(("groups", "ctx"), None),
            P(),
            P(),
            P(None, "ctx"),
            P(None, "ctx"),
            P("ctx", None),
            P("groups"),
            P("groups"),
            P(("groups", "ctx"), None),
            P("groups", None),
        ),
        out_specs=P(("groups", "ctx"), None),
        check_vma=False,
    )
```

profile of v0, /device:TPU:0, one launch (start us, length us, event | category | flops | bytes accessed | tf_op | source)
XLA Modules:
  0.0 280.0 jit_solution(8424827407678132025)
XLA Ops:
  6.5 0.0 copy-start
  6.5 0.0 all-gather.2.cloned.1.call-start
  6.5 0.9 broadcast_compare_fusion
  7.4 0.8 dynamic_slice.10
  8.2 0.8 dynamic_slice.9
  8.9 0.9 copy.18
  9.8 24.6 %all_gather.10 = bf16[2048,128]{0,1:T(8,128)(2,1)S(1)} all-gather(bf16[128,128]{0,1:T(8,128)(2,1)S(1)} %copy.18), channel_id=1, replica_groups=mesh['groups'=2,'ctx'=16] {'ctx'}, dimensions={0}, use_global_device_ids=true | all-gather | bytes 557056 | tf_op jit(solution)/shard_map/all_gather | solution.py:36
  34.4 19.1 %all_gather.9 = bf16[2048,128]{1,0:T(8,128)(2,1)S(1)} all-gather(bf16[128,128]{1,0:T(8,128)(2,1)} %param.15), channel_id=1, replica_groups=mesh['groups'=2,'ctx'=16] {'ctx'}, dimensions={0}, use_global_device_ids=true | all-gather | bytes 557056 | tf_op jit(solution)/shard_map/all_gather | solution.py:35
  53.5 3.1 %fusion.13 = pred[128,2048]{0,1:T(8,128)(4,1)S(1)} fusion(s32[128]{0:T(128)S(1)} %dynamic_slice.10, s32[128]{0:T(128)S(1)} %iota_add_fusion, s32[128]{0:T(128)S(1)} %dynamic_slice.9, s32[2048]{0:T(1024)} %param.23, s32[2048]{0:T(1024)} %param.22, pred[2048]{0:T(1024)(128)(4,1)S(1)} %broadcast_compare_fusion), kind=kLoop, calls=%fused_computation.20 | loop fusion | flops 1572864 | bytes 282112 | tf_op jit(solution)/shard_map/and | solution.py:40
  56.6 2.3 fusion
  58.9 2.0 fusion.1
  60.9 0.0 copy-start.2
  60.9 0.0 copy-start.3
  61.0 0.0 copy-start.4
  61.0 2.2 fusion.17
  63.2 0.0 copy-done.2
  63.2 0.0 copy-done.3
  63.2 0.8 multiply_reduce_fusion
  64.1 0.0 copy-start.1
  64.1 1.0 copy-done.1
  65.0 0.0 copy-done.4
  65.0 1.0 multiply_convert_fusion.1
  66.0 0.0 all-gather.2.cloned.1.call-update
  66.0 0.2 reduce-scatter.2.cloned.1.call-start
  66.2 72.6 %all-gather.2.cloned.1.call-done = bf16[2048,2048]{1,0:T(8,128)(2,1)} async-done(((bf16[128,2048]{1,0:T(8,128)(2,1)}), bf16[2048,2048]{1,0:T(8,128)(2,1)}) %all-gather.2.cloned.1.call-update) | async-done | bytes 8388624 | tf_op jit(solution)/shard_map/all_gather | solution.py:78
  138.8 11.0 %fusion.32 = f32[2048,688]{0,1:T(8,128)} fusion(bf16[2048,2048]{1,0:T(8,128)(2,1)} %all-gather.2.cloned.1.call-done, bf16[2048,688]{0,1:T(8,128)(2,1)} %param.19), kind=kOutput, calls=%fused_computation.43 | convolution fusion | flops 5771362304 | bytes 16842752 | tf_op jit(solution)/shard_map/dot_general | solution.py:79
  149.8 0.0 copy-done
  149.8 18.9 %convolution_convert_fusion = bf16[2048,2048]{1,0:T(8,128)(2,1)} fusion(bf16[688,2048]{1,0:T(8,128)(2,1)S(1)} %copy-done, f32[2048,688]{0,1:T(8,128)} %fusion.32, bf16[2048,2048]{1,0:T(8,128)(2,1)} %all-gather.2.cloned.1.call-done, bf16[2048,688]{0,1:T(8,128)(2,1)} %param.20), kind=kOutput, calls=%fused_computation.3 | convolution fusion | flops 11555373056 | bytes 28049408 | tf_op jit(solution)/shard_map/dot_general | solution.py:83
  168.7 0.0 copy-start.5
  168.7 0.0 reduce-scatter.2.cloned.1.call-update
  168.7 0.7 dynamic-slice_bitcast_fusion
  169.4 0.1 iota_compare_fusion.1
  169.5 0.1 lt.36
  169.5 0.0 copy-done.5
  169.6 1.0 scatter_custom_fusion
  170.6 100.3 %reduce-scatter.2.cloned.1.call-done = bf16[128,2048]{1,0:T(8,128)(2,1)} async-done(((bf16[2048,2048]{1,0:T(8,128)(2,1)}), bf16[128,2048]{1,0:T(8,128)(2,1)}) %reduce-scatter.2.cloned.1.call-update) | async-done | bytes 524304 | tf_op jit(solution)/shard_map/reduce_scatter | solution.py:82
  270.9 2.3 add_convert_fusion
  (5 shorter events, 0.0 us)
Async XLA Ops:
  6.5 143.2 %copy-start = (bf16[688,2048]{1,0:T(8,128)(2,1)S(1)}, bf16[688,2048]{1,0:T(8,128)(2,1)}, u32[]{:S(2)}) copy-start(bf16[688,2048]{1,0:T(8,128)(2,1)} %param.21) | copy-start | bytes 8454148
  6.5 132.3 %all-gather.2.cloned.1.call-start = ((), (), s32[]{:S(2)}) async-start(), calls=%async_computation.1 | async-start | bytes 8912896 | tf_op jit(solution)/shard_map/all_gather | solution.py:78
  60.9 2.3 copy-start.2
  60.9 2.3 copy-start.3
  61.0 4.1 %copy-start.4 = (f32[2048]{0:T(1024)S(1)}, f32[2048]{0:T(1024)}, u32[]{:S(2)}) copy-start(f32[2048]{0:T(1024)} %param.18) | copy-start | bytes 24580
  64.1 1.0 copy-start.1
  66.0 204.8 %reduce-scatter.2.cloned.1.call-start = ((), (), s32[]{:S(2)}) async-start(), calls=%async_computation.2 | async-start | bytes 8912896 | tf_op jit(solution)/shard_map/reduce_scatter | solution.py:82
  168.7 0.9 copy-start.5
Sparse Core Ops, SparseCore 0:
  66.1 72.6 all-gather.1
  168.8 102.0 reduce-scatter.1
where the time goes:
time: 280 us
  waiting for transfers between devices  173 us (62%)
  blocking collectives  43.7 us (16%)
  matrix products  35.2 us (13%)
  between operations  13.5 us (5%)
  other arithmetic  9.31 us (3%)
  local copies, waits for them, and re-layouts  5.19 us (2%)
    reduce_scatter x1, waiting for transfers between devices, on_device(): lax.psum_scatter(jnp.dot(inner_out, down_weight, preferred_element_type=j...  100 us
    all_gather x1, waiting for transfers between devices, on_device(): gathered = lax.all_gather(normed, 'ctx', axis=0, tiled=True)  72.6 us
    all_gather x1, blocking collectives, on_device(): value_piece = lax.all_gather(values, 'ctx', axis=0, tiled=True)  24.6 us
    all_gather x1, blocking collectives, on_device(): key_piece = lax.all_gather(keys, 'ctx', axis=0, tiled=True)  19.1 us
    dot_general x1, matrix products, on_device(): jnp.dot(inner_out, down_weight, preferred_element_type=jnp.float32)  18.9 us
    dot_general x1, matrix products, on_device(): jnp.dot(gathered, gate_weight, preferred_element_type=jnp.float32)  11 us
  transfers between devices with their start and end apart: 2, of which 2 were waited for; matrix products, arithmetic and copies ran while one was open for 1% of the time, Pallas kernels for 0%

commit v1 on v0

--- a/solution.py
+++ b/solution.py
@@ -1,9 +1,363 @@
+import functools
+
 import jax
 import jax.numpy as jnp
 from jax import lax
+from jax.experimental import pallas as pl
+from jax.experimental.pallas import tpu as pltpu
 from jax.sharding import PartitionSpec as P
 
 NEG_FILL = -1e30
+MESH = pl.DeviceIdType.MESH
+PLANES = 2
+CORES = 2
+DOWN_TILE = 512
+
+
+def place(n):
+    me = lax.axis_index("ctx")
+    return me, me // (PLANES * CORES), (me // CORES) % PLANES, me % CORES
+
+
+def index_of(z, y, c):
+    return (z * PLANES + y) * CORES + c
+
+
+def near_first(z, i, stages):
+    short = jnp.minimum(z, stages - 1 - z)
+    step = (i + 1) // 2
+    inner = jnp.where(i % 2 == 1, z + step, z - step)
+    outer = jnp.where(z < stages - 1 - z, z + i - short, z - i + short)
+    return jnp.where(i <= 2 * short, inner, outer)
+
+
+def greet(n):
+    me, z, y, c = place(n)
+    stages = n // (PLANES * CORES)
+    barrier = pltpu.get_barrier_semaphore()
+
+    def hello(target):
+        pl.semaphore_signal(barrier, inc=1, device_id={"ctx": target}, device_id_type=MESH)
+
+    hello(index_of(z, 1 - y, c))
+    hello(index_of(z, y, 1 - c))
+    pl.when(z > 0)(lambda: hello(index_of(z - 1, y, c)))
+    pl.when(z < stages - 1)(lambda: hello(index_of(z + 1, y, c)))
+    pl.semaphore_wait(barrier, 2 + (z > 0).astype(jnp.int32) + (z < stages - 1).astype(jnp.int32))
+
+
+def remote(src, dst, send_sem, recv_sem, target):
+    return pltpu.make_async_remote_copy(
+        src_ref=src,
+        dst_ref=dst,
+        send_sem=send_sem,
+        recv_sem=recv_sem,
+        device_id={"ctx": target},
+        device_id_type=MESH,
+    )
+
+
+class Spread:
+    def __init__(self, n, rows, full, send, recv):
+        self.n, self.rows, self.full, self.send, self.recv = n, rows, full, send, recv
+        self.me, self.z, self.y, self.c = place(n)
+        self.stages = n // (PLANES * CORES)
+
+    def block(self, b):
+        return self.full.at[pl.ds(pl.multiple_of(b * self.rows, self.rows), self.rows)]
+
+    def copy(self, b, way, target):
+        return remote(
+            self.block(b), self.block(b), self.send.at[b, way], self.recv.at[b], target
+        )
+
+    def wait_for(self, b):
+        self.copy(b, 0, index_of(self.z, self.y, 1 - self.c)).wait_recv()
+
+    def ways(self, i, act):
+        z, y, c = self.z, self.y, self.c
+        far = near_first(z, i, self.stages)
+        b = index_of(far, y, c)
+        act(self.copy(b, 0, index_of(z, 1 - y, c)))
+        pl.when((z < self.stages - 1) & (far <= z))(
+            lambda: act(self.copy(b, 1, index_of(z + 1, y, c)))
+        )
+        pl.when((z > 0) & (far >= z))(lambda: act(self.copy(b, 2, index_of(z - 1, y, c))))
+        act(self.copy(b, 3, index_of(z, y, 1 - c)))
+
+    def start_own(self, i):
+        pl.when(i > 0)(
+            lambda: self.wait_for(index_of(near_first(self.z, i, self.stages), self.y, self.c))
+        )
+        self.ways(i, lambda copy: copy.start())
+
+    def cross(self, i):
+        b = index_of(near_first(self.z, i, self.stages), 1 - self.y, self.c)
+        return b, self.copy(b, 3, index_of(self.z, self.y, 1 - self.c))
+
+    def start_cross(self, i):
+        b, copy = self.cross(i)
+        self.wait_for(b)
+        copy.start()
+
+    def finish(self):
+        def body(i, carry):
+            self.ways(i, lambda copy: copy.wait_send())
+            self.cross(i)[1].wait_send()
+            return carry
+
+        lax.fori_loop(0, self.stages, body, 0)
+
+
+def gather_kernel(n, x_ref, full, send, recv, own_sem):
+    spread = Spread(n, x_ref.shape[0], full, send, recv)
+    own = pltpu.make_async_copy(x_ref, spread.block(spread.me), own_sem)
+    own.start()
+    greet(n)
+    own.wait()
+    spread.start_own(0)
+
+    def body(i, carry):
+        pl.when(i + 1 < spread.stages)(lambda: spread.start_own(i + 1))
+        spread.start_cross(i)
+        return carry
+
+    lax.fori_loop(0, spread.stages, body, 0)
+
+    def arrive(i, carry):
+        spread.wait_for(index_of(i // PLANES, i % PLANES, 1 - spread.c))
+        return carry
+
+    lax.fori_loop(0, n // CORES, arrive, 0)
+    spread.finish()
+
+
+def gather_rows(n, x):
+    rows, width = x.shape
+    return pl.pallas_call(
+        functools.partial(gather_kernel, n),
+        out_shape=jax.ShapeDtypeStruct((n * rows, width), x.dtype),
+        in_specs=[pl.BlockSpec(memory_space=pltpu.VMEM)],
+        out_specs=pl.BlockSpec(memory_space=pltpu.VMEM),
+        scratch_shapes=[
+            pltpu.SemaphoreType.DMA((n, 4)),
+            pltpu.SemaphoreType.DMA((n,)),
+            pltpu.SemaphoreType.DMA,
+        ],
+        compiler_params=pltpu.CompilerParams(collective_id=0, has_side_effects=True),
+    )(x)
+
+
+def ffn_kernel(
+    n,
+    x_hbm,
+    gate_hbm,
+    up_hbm,
+    down_hbm,
+    out_ref,
+    full,
+    gate,
+    up,
+    down,
+    part,
+    from_core,
+    from_plane,
+    from_stage,
+    send,
+    recv,
+    core_send,
+    core_recv,
+    plane_send,
+    plane_recv,
+    stage_send,
+    stage_recv,
+    local_sem,
+):
+    rows = x_hbm.shape[0]
+    width = x_hbm.shape[1]
+    spread = Spread(n, rows, full, send, recv)
+    me, z, y, c = spread.me, spread.z, spread.y, spread.c
+    stages = spread.stages
+    own = pltpu.make_async_copy(x_hbm, spread.block(me), local_sem.at[0])
+    own.start()
+    weights = [
+        pltpu.make_async_copy(gate_hbm, gate, local_sem.at[1]),
+        pltpu.make_async_copy(up_hbm, up, local_sem.at[2]),
+        pltpu.make_async_copy(down_hbm, down, local_sem.at[3]),
+    ]
+    greet(n)
+    own.wait()
+    spread.start_own(0)
+    for copy in weights:
+        copy.start()
+
+    def span(b):
+        return pl.ds(pl.multiple_of(b * rows, rows), rows)
+
+    def chip_of(k):
+        far = near_first(z, k // 2, stages)
+        return far, jnp.where(k % 2 == 0, y, 1 - y)
+
+    def core_copy(chip):
+        theirs = span(chip * CORES + 1 - c)
+        return remote(
+            part.at[theirs],
+            from_core.at[span(chip)],
+            core_send.at[chip],
+            core_recv.at[chip],
+            index_of(z, y, 1 - c),
+        )
+
+    def plane_copy(far):
+        return remote(
+            part.at[span(index_of(far, 1 - y, c))],
+            from_plane.at[span(far)],
+            plane_send.at[far],
+            plane_recv.at[far],
+            index_of(z, 1 - y, c),
+        )
+
+    def stage_copy(far, slot, target):
+        return remote(
+            part.at[span(index_of(far, y, c))],
+            from_stage.at[span(slot)],
+            stage_send.at[far],
+            stage_recv.at[slot],
+            target,
+        )
+
+    def wide(ref, where):
+        return ref[where, :].astype(jnp.float32)
+
+    def join_cores(k):
+        far, plane = chip_of(k)
+        chip = far * PLANES + plane
+        core_copy(chip).wait_recv()
+        mine = span(chip * CORES + c)
+        part[mine, :] = (wide(part, mine) + wide(from_core, span(chip))).astype(part.dtype)
+        pl.when(k % 2 == 1)(lambda: plane_copy(far).start())
+
+    def step(k, carry):
+        i = k // 2
+
+        @pl.when(k % 2 == 1)
+        def _():
+            pl.when(i + 1 < stages)(lambda: spread.start_own(i + 1))
+            spread.start_cross(i)
+
+        far, plane = chip_of(k)
+        chip = far * PLANES + plane
+        spread.wait_for(chip * CORES + 1 - c)
+
+        @pl.when(k == 0)
+        def _():
+            for copy in weights:
+                copy.wait()
+
+        both = pl.ds(pl.multiple_of(chip * CORES * rows, CORES * rows), CORES * rows)
+        x = full[both, :]
+        gate_out = jnp.dot(x, gate[...], preferred_element_type=jnp.float32)
+        up_out = jnp.dot(x, up[...], preferred_element_type=jnp.float32)
+        inner = (gate_out / (1.0 + jnp.exp(-gate_out)) * up_out).astype(jnp.bfloat16)
+        tile = DOWN_TILE if width % DOWN_TILE == 0 else width
+        for at in range(0, width, tile):
+            part[both, at : at + tile] = jnp.dot(
+                inner, down[:, at : at + tile], preferred_element_type=jnp.float32
+            ).astype(part.dtype)
+        core_copy(chip).start()
+        pl.when(k > 0)(lambda: join_cores(k - 1))
+        return carry
+
+    lax.fori_loop(0, PLANES * stages, step, 0)
+    join_cores(PLANES * stages - 1)
+
+    def chain(j, carry):
+        far = near_first(z, stages - 1 - j, stages)
+        down_way = far < z
+        slot = jnp.where(down_way, far, far + 1)
+        target = index_of(jnp.where(down_way, z - 1, z + 1), y, c)
+        fed = jnp.where(down_way, z < stages - 1, z > 0)
+        mine = span(index_of(far, y, c))
+        plane_copy(far).wait_recv()
+        copy = stage_copy(far, slot, target)
+
+        @pl.when(fed)
+        def _():
+            copy.wait_recv()
+            part[mine, :] = (
+                wide(part, mine) + wide(from_plane, span(far)) + wide(from_stage, span(slot))
+            ).astype(part.dtype)
+
+        @pl.when(jnp.logical_not(fed))
+        def _():
+            part[mine, :] = (wide(part, mine) + wide(from_plane, span(far))).astype(part.dtype)
+
+        copy.start()
+        return carry
+
+    lax.fori_loop(0, stages - 1, chain, 0)
+
+    plane_copy(z).wait_recv()
+    mine = span(me)
+    out_ref[...] = wide(part, mine) + wide(from_plane, span(z))
+
+    @pl.when(z < stages - 1)
+    def _():
+        stage_copy(z, z, index_of(z, 1 - y, c)).wait_recv()
+        out_ref[...] += wide(from_stage, span(z))
+
+    @pl.when(z > 0)
+    def _():
+        stage_copy(z, z + 1, index_of(z, 1 - y, c)).wait_recv()
+        out_ref[...] += wide(from_stage, span(z + 1))
+
+    def settle(i, carry):
+        core_copy(i).wait_send()
+        return carry
+
+    lax.fori_loop(0, PLANES * stages, settle, 0)
+
+    def settle_stage(i, carry):
+        plane_copy(i).wait_send()
+        pl.when(i != z)(lambda: stage_copy(i, i, index_of(z, 1 - y, c)).wait_send())
+        return carry
+
+    lax.fori_loop(0, stages, settle_stage, 0)
+    spread.finish()
+
+
+def feed_forward(n, x, gate_weight, up_weight, down_weight):
+    rows, width = x.shape
+    stages = n // (PLANES * CORES)
+    bf16 = jnp.bfloat16
+    return pl.pallas_call(
+        functools.partial(ffn_kernel, n),
+        out_shape=jax.ShapeDtypeStruct((rows, width), jnp.float32),
+        in_specs=[pl.BlockSpec(memory_space=pl.ANY)] * 4,
+        out_specs=pl.BlockSpec(memory_space=pltpu.VMEM),
+        scratch_shapes=[
+            pltpu.VMEM((n * rows, width), bf16),
+            pltpu.VMEM(gate_weight.shape, bf16),
+            pltpu.VMEM(up_weight.shape, bf16),
+            pltpu.VMEM(down_weight.shape, bf16),
+            pltpu.VMEM((n * rows, width), bf16),
+            pltpu.VMEM((n // CORES * rows, width), bf16),
+            pltpu.VMEM((stages * rows, width), bf16),
+            pltpu.VMEM(((stages + 1) * rows, width), bf16),
+            pltpu.SemaphoreType.DMA((n, 4)),
+            pltpu.SemaphoreType.DMA((n,)),
+            pltpu.SemaphoreType.DMA((n // CORES,)),
+            pltpu.SemaphoreType.DMA((n // CORES,)),
+            pltpu.SemaphoreType.DMA((stages,)),
+            pltpu.SemaphoreType.DMA((stages,)),
+            pltpu.SemaphoreType.DMA((stages,)),
+            pltpu.SemaphoreType.DMA((stages + 1,)),
+            pltpu.SemaphoreType.DMA((4,)),
+        ],
+        compiler_params=pltpu.CompilerParams(
+            collective_id=1, has_side_effects=True, vmem_limit_bytes=64 * 1000 * 1000
+        ),
+    )(x, gate_weight, up_weight, down_weight)
 
 
 def on_device(
@@ -32,8 +386,8 @@
     query_role = lax.dynamic_slice_in_dim(roles, own_begin, tok_rows)
     query_heads = queries.reshape(tok_rows, head_count, head_dim)
     score_scale = 1.0 / head_dim**0.5
-    key_piece = lax.all_gather(keys, "ctx", axis=0, tiled=True)
-    value_piece = lax.all_gather(values, "ctx", axis=0, tiled=True)
+    both = gather_rows(devices, jnp.concatenate([keys, values], axis=1))
+    key_piece, value_piece = both[:, :head_dim], both[:, head_dim:]
     row_count = key_piece.shape[0]
     key_pos = jnp.arange(row_count, dtype=jnp.int32)
     seen_mask = (
@@ -75,18 +429,9 @@
         my_counts, capacity
     )
     target = jnp.where(valid, rows_flat, tok_rows)
-    gathered = lax.all_gather(normed, "ctx", axis=0, tiled=True)
-    gate_out = jnp.dot(gathered, gate_weight, preferred_element_type=jnp.float32)
-    up_out = jnp.dot(gathered, up_weight, preferred_element_type=jnp.float32)
-    inner_out = (jax.nn.silu(gate_out) * up_out).astype(jnp.bfloat16)
-    summed = lax.psum_scatter(
-        jnp.dot(inner_out, down_weight, preferred_element_type=jnp.float32).astype(jnp.bfloat16),
-        "ctx",
-        scatter_dimension=0,
-        tiled=True,
-    )
+    summed = feed_forward(devices, normed, gate_weight, up_weight, down_weight)
     live_mask = jnp.zeros((tok_rows,), jnp.float32).at[target].set(1.0, mode="drop")
-    ffn_round = lax.optimization_barrier(summed)
+    ffn_round = lax.optimization_barrier(summed.astype(jnp.bfloat16))
     ffn_back = ffn_round.astype(jnp.float32) * live_mask[:, None]
     return (residual.astype(jnp.float32) + ffn_back).astype(jnp.bfloat16)
 

time: 280 us -> 183 us (0.65)
  waiting for transfers between devices: 173 us -> 0 us
  Pallas kernels: 0 us -> 154 us
  blocking collectives: 43.7 us -> 0 us
  matrix products: 35.2 us -> 5.37 us
  between operations: 13.5 us -> 0.16 us
  local copies, waits for them, and re-layouts: 5.19 us -> 12.8 us
    pallas_call x0 -> x2, Pallas kernels: none -> 154 us  [the longest x1 133 us: feed_forward(): pl.pallas_call(functools.partial(ffn_kernel, n), out_shape=jax.ShapeDtype...]
    reduce_scatter x1 -> x0, waiting for transfers between devices: 100 us -> none  [on_device(): lax.psum_scatter(jnp.dot(inner_out, down_weight, preferred_element_type=j...]
    all_gather x1 -> x0, waiting for transfers between devices: 72.6 us -> none  [on_device(): gathered = lax.all_gather(normed, 'ctx', axis=0, tiled=True)]
    all_gather x2 -> x0, blocking collectives: 43.7 us -> none  [the longest x1 24.6 us: on_device(): value_piece = lax.all_gather(values, 'ctx', axis=0, tiled=True)]
    dot_general x2 -> x0, matrix products: 29.8 us -> none  [the longest x1 18.9 us: on_device(): jnp.dot(inner_out, down_weight, preferred_element_type=jnp.float32)]
    unnamed x13 -> x14, local copies, waits for them, and re-layouts: 1.9 us -> 9.44 us
  transfers between devices with their start and end apart: 2 -> 0, of which waited for: 2 -> 0; matrix products, arithmetic and copies ran while one was open for 1% -> 0% of each run, Pallas kernels for 0% -> 0%
where the time goes in v1:
time: 183 us; the launch traced here: 182 us
  Pallas kernels  154 us (84%)
  local copies, waits for them, and re-layouts  12.8 us (7%)
  other arithmetic  10.5 us (6%)
  matrix products  5.37 us (3%)
    pallas_call x1, Pallas kernels, feed_forward(): pl.pallas_call(functools.partial(ffn_kernel, n), out_shape=jax.ShapeDtype...  133 us
    pallas_call x1, Pallas kernels, gather_rows(): pl.pallas_call(functools.partial(gather_kernel, n), out_shape=jax.ShapeDt...  20.7 us
    unnamed x14, local copies, waits for them, and re-layouts  9.44 us

profile of v1, /device:TPU:0, one launch (start us, length us, event | category | flops | bytes accessed | tf_op | source)
XLA Modules:
  0.0 182.4 jit_solution(11314792257609863685)
XLA Ops:
  0.0 0.0 copy-start
  0.0 0.8 dynamic_slice.10
  0.8 0.8 dynamic_slice.9
  1.6 0.7 broadcast_compare_fusion
  2.3 3.1 %fusion.12 = pred[128,2048]{0,1:T(8,128)(4,1)S(1)} fusion(s32[128]{0:T(128)S(1)} %dynamic_slice.10, s32[128]{0:T(128)S(1)} %iota_add_fusion, s32[128]{0:T(128)S(1)} %dynamic_slice.9, s32[2048]{0:T(1024)} %param.23, s32[2048]{0:T(1024)} %param.22, pred[2048]{0:T(1024)(128)(4,1)S(1)} %broadcast_compare_fusion), kind=kLoop, calls=%fused_computation.17 | loop fusion | flops 1572864 | bytes 282112 | tf_op jit(solution)/shard_map/and | solution.py:394
  5.3 1.4 pad_maximum_fusion.x_ref
  6.8 20.7 %shard_map.127 = bf16[2048,256]{1,0:T(8,128)(2,1)} custom-call(bf16[128,256]{1,0:T(8,128)(2,1)} %pad_maximum_fusion.x_ref), custom_call_target="tpu_custom_call" | custom-call | tf_op jit(solution)/shard_map/pallas_call | solution.py:137
  27.5 0.0 copy-done
  27.5 0.0 copy-start.2
  27.5 2.5 %fusion = (f32[8,128]{1,0:T(8,128)S(1)}, f32[2048,128,8]{1,0,2:T(8,128)S(1)}) fusion(pred[128,2048]{0,1:T(8,128)(4,1)S(1)} %fusion.12, bf16[2048,256]{1,0:T(8,128)(2,1)} %shard_map.127, bf16[128,1024]{1,0:T(8,128)(2,1)S(1)} %copy-done), kind=kOutput, calls=%fused_computation.3 | convolution fusion | flops 543161344 | bytes 9441280 | tf_op jit(solution)/shard_map/tqd,kd->qtk/dot_general | solution.py:400
  30.0 2.0 %fusion.1 = f32[8,128]{1,0:T(8,128)S(1)} fusion(f32[2048,128,8]{1,0,2:T(8,128)S(1)} %get-tuple-element.6, f32[8,128]{1,0:T(8,128)S(1)} %broadcast_maximum_fusion, pred[128,2048]{0,1:T(8,128)(4,1)S(1)} %fusion.12), kind=kLoop, calls=%fused_computation.4 | loop fusion | flops 10484736 | bytes 8658944 | tf_op jit(solution)/shard_map/reduce_sum | solution.py:406
  32.0 0.0 copy-done.2
  32.0 0.0 copy-start.1
  32.1 0.0 copy-start.3
  32.1 0.0 copy-start.4
  32.1 2.1 %fusion.16 = bf16[128,8,128]{0,2,1:T(8,128)(2,1)S(1)} fusion(f32[2048,128,8]{1,0,2:T(8,128)S(1)} %get-tuple-element.6, f32[8,128]{1,0:T(8,128)S(1)} %broadcast_maximum_fusion, pred[128,2048]{0,1:T(8,128)(4,1)S(1)} %fusion.12, bf16[2048,256]{1,0:T(8,128)(2,1)S(1)} %copy-done.2, f32[128,8]{0,1:T(8,128)S(1)} %bitcast.53), kind=kOutput, calls=%fused_computation.19 | convolution fusion | flops 547618816 | bytes 9445376 | tf_op jit(solution)/shard_map/qtk,kd->qtd/dot_general | solution.py:407
  34.2 0.1 copy-done.1
  34.2 0.1 copy-done.3
  34.4 0.8 multiply_reduce_fusion
  35.2 0.0 copy-done.4
  35.2 1.0 multiply_convert_fusion.x_hbm
  36.1 4.6 %copy.22.gate_hbm = bf16[2048,688]{1,0:T(8,128)(2,1)} copy(bf16[2048,688]{0,1:T(8,128)(2,1)} %param.19) | data formatting | bytes 5636096 | tf_op args[6]
  40.7 0.0 copy-start.5
  40.7 4.6 %copy.23.up_hbm = bf16[2048,688]{1,0:T(8,128)(2,1)} copy(bf16[2048,688]{0,1:T(8,128)(2,1)} %param.20) | data formatting | bytes 5636096 | tf_op args[7]
  45.4 132.9 %shard_map.128 = f32[128,2048]{1,0:T(8,128)} custom-call(bf16[128,2048]{1,0:T(8,128)(2,1)} %multiply_convert_fusion.x_hbm, bf16[2048,688]{1,0:T(8,128)(2,1)} %copy.22.gate_hbm, bf16[2048,688]{1,0:T(8,128)(2,1)} %copy.23.up_hbm, bf16[688,2048]{1,0:T(8,128)(2,1)} %down_hbm.1), custom_call_target="tpu_custom_call" | custom-call | tf_op jit(solution)/shard_map/pallas_call | solution.py:333
  178.2 1.3 convert_element_type.38
  179.5 0.7 dynamic-slice_bitcast_fusion
  180.2 0.1 iota_compare_fusion.1
  180.3 0.1 lt.36
  180.4 0.0 copy-done.5
  180.4 1.0 scatter_custom_fusion
  181.4 1.0 add_convert_fusion
  (5 shorter events, 0.0 us)
Async XLA Ops:
  0.0 27.5 %copy-start = (bf16[128,1024]{1,0:T(8,128)(2,1)S(1)}, bf16[128,1024]{1,0:T(8,128)(2,1)}, u32[]{:S(2)}) copy-start(bf16[128,1024]{1,0:T(8,128)(2,1)} %param.14) | copy-start | bytes 786436
  27.5 4.5 %copy-start.2 = (bf16[2048,256]{1,0:T(8,128)(2,1)S(1)}, bf16[2048,256]{1,0:T(8,128)(2,1)}, u32[]{:S(2)}) copy-start(bf16[2048,256]{1,0:T(8,128)(2,1)} %shard_map.127) | copy-start | bytes 3145732
  32.0 2.2 %copy-start.1 = (bf16[1024,2048]{1,0:T(8,128)(2,1)S(1)}, bf16[1024,2048]{1,0:T(8,128)(2,1)}, u32[]{:S(2)}) copy-start(bf16[1024,2048]{1,0:T(8,128)(2,1)} %param.17) | copy-start | bytes 12582916
  32.1 2.3 %copy-start.3 = (bf16[128,2048]{1,0:T(8,128)(2,1)S(1)}, bf16[128,2048]{1,0:T(8,128)(2,1)}, u32[]{:S(2)}) copy-start(bf16[128,2048]{1,0:T(8,128)(2,1)} %param.13) | copy-start | bytes 1572868
  32.1 3.1 %copy-start.4 = (f32[2048]{0:T(1024)S(1)}, f32[2048]{0:T(1024)}, u32[]{:S(2)}) copy-start(f32[2048]{0:T(1024)} %param.18) | copy-start | bytes 24580
  40.7 139.7 %copy-start.5 = (s32[1,128]{1,0:T(1,128)S(1)}, s32[1,128]{1,0:T(1,128)}, u32[]{:S(2)}) copy-start(s32[1,128]{1,0:T(1,128)} %param.24) | copy-start | bytes 1540

commit v2 on v1

--- a/solution.py
+++ b/solution.py
@@ -12,6 +12,7 @@
 PLANES = 2
 CORES = 2
 DOWN_TILE = 512
+PIECES = 2
 
 
 def place(n):
@@ -58,7 +59,8 @@
 
 
 class Spread:
-    def __init__(self, n, rows, full, send, recv):
+    def __init__(self, n, rows, full, send, recv, pieces=1):
+        self.pieces, self.piece_rows = pieces, rows // pieces
         self.n, self.rows, self.full, self.send, self.recv = n, rows, full, send, recv
         self.me, self.z, self.y, self.c = place(n)
         self.stages = n // (PLANES * CORES)
@@ -66,44 +68,50 @@
     def block(self, b):
         return self.full.at[pl.ds(pl.multiple_of(b * self.rows, self.rows), self.rows)]
 
-    def copy(self, b, way, target):
-        return remote(
-            self.block(b), self.block(b), self.send.at[b, way], self.recv.at[b], target
-        )
+    def copy(self, b, way, target, p):
+        begin = pl.multiple_of(b * self.rows + p * self.piece_rows, self.piece_rows)
+        piece = self.full.at[pl.ds(begin, self.piece_rows)]
+        return remote(piece, piece, self.send.at[b, way, p], self.recv.at[b, p], target)
+
+    def wait_piece(self, b, p):
+        self.copy(b, 0, index_of(self.z, self.y, 1 - self.c), p).wait_recv()
 
     def wait_for(self, b):
-        self.copy(b, 0, index_of(self.z, self.y, 1 - self.c)).wait_recv()
-
-    def ways(self, i, act):
+        for p in range(self.pieces):
+            self.wait_piece(b, p)
+
+    def ways(self, i, p, act):
         z, y, c = self.z, self.y, self.c
         far = near_first(z, i, self.stages)
         b = index_of(far, y, c)
-        act(self.copy(b, 0, index_of(z, 1 - y, c)))
+        act(self.copy(b, 0, index_of(z, 1 - y, c), p))
         pl.when((z < self.stages - 1) & (far <= z))(
-            lambda: act(self.copy(b, 1, index_of(z + 1, y, c)))
+            lambda: act(self.copy(b, 1, index_of(z + 1, y, c), p))
         )
-        pl.when((z > 0) & (far >= z))(lambda: act(self.copy(b, 2, index_of(z - 1, y, c))))
-        act(self.copy(b, 3, index_of(z, y, 1 - c)))
+        pl.when((z > 0) & (far >= z))(lambda: act(self.copy(b, 2, index_of(z - 1, y, c), p)))
+        act(self.copy(b, 3, index_of(z, y, 1 - c), p))
 
     def start_own(self, i):
-        pl.when(i > 0)(
-            lambda: self.wait_for(index_of(near_first(self.z, i, self.stages), self.y, self.c))
-        )
-        self.ways(i, lambda copy: copy.start())
-
-    def cross(self, i):
+        b = index_of(near_first(self.z, i, self.stages), self.y, self.c)
+        for p in range(self.pieces):
+            pl.when(i > 0)(functools.partial(self.wait_piece, b, p))
+            self.ways(i, p, lambda copy: copy.start())
+
+    def cross(self, i, p):
         b = index_of(near_first(self.z, i, self.stages), 1 - self.y, self.c)
-        return b, self.copy(b, 3, index_of(self.z, self.y, 1 - self.c))
+        return b, self.copy(b, 3, index_of(self.z, self.y, 1 - self.c), p)
 
     def start_cross(self, i):
-        b, copy = self.cross(i)
-        self.wait_for(b)
-        copy.start()
+        for p in range(self.pieces):
+            b, copy = self.cross(i, p)
+            self.wait_piece(b, p)
+            copy.start()
 
     def finish(self):
         def body(i, carry):
-            self.ways(i, lambda copy: copy.wait_send())
-            self.cross(i)[1].wait_send()
+            for p in range(self.pieces):
+                self.ways(i, p, lambda copy: copy.wait_send())
+                self.cross(i, p)[1].wait_send()
             return carry
 
         lax.fori_loop(0, self.stages, body, 0)
@@ -140,8 +148,8 @@
         in_specs=[pl.BlockSpec(memory_space=pltpu.VMEM)],
         out_specs=pl.BlockSpec(memory_space=pltpu.VMEM),
         scratch_shapes=[
-            pltpu.SemaphoreType.DMA((n, 4)),
-            pltpu.SemaphoreType.DMA((n,)),
+            pltpu.SemaphoreType.DMA((n, 4, 1)),
+            pltpu.SemaphoreType.DMA((n, 1)),
             pltpu.SemaphoreType.DMA,
         ],
         compiler_params=pltpu.CompilerParams(collective_id=0, has_side_effects=True),
@@ -175,7 +183,7 @@
 ):
     rows = x_hbm.shape[0]
     width = x_hbm.shape[1]
-    spread = Spread(n, rows, full, send, recv)
+    spread = Spread(n, rows, full, send, recv, PIECES)
     me, z, y, c = spread.me, spread.z, spread.y, spread.c
     stages = spread.stages
     own = pltpu.make_async_copy(x_hbm, spread.block(me), local_sem.at[0])
@@ -217,12 +225,17 @@
             index_of(z, 1 - y, c),
         )
 
-    def stage_copy(far, slot, target):
+    piece_rows = rows // PIECES
+
+    def piece(b, p):
+        return pl.ds(pl.multiple_of(b * rows + p * piece_rows, piece_rows), piece_rows)
+
+    def stage_copy(far, slot, target, p):
         return remote(
-            part.at[span(index_of(far, y, c))],
-            from_stage.at[span(slot)],
-            stage_send.at[far],
-            stage_recv.at[slot],
+            part.at[piece(index_of(far, y, c), p)],
+            from_stage.at[piece(slot, p)],
+            stage_send.at[far, p],
+            stage_recv.at[slot, p],
             target,
         )
 
@@ -256,8 +269,9 @@
 
         both = pl.ds(pl.multiple_of(chip * CORES * rows, CORES * rows), CORES * rows)
         x = full[both, :]
-        gate_out = jnp.dot(x, gate[...], preferred_element_type=jnp.float32)
-        up_out = jnp.dot(x, up[...], preferred_element_type=jnp.float32)
+        turned = (((1,), (1,)), ((), ()))
+        gate_out = lax.dot_general(x, gate[...], turned, preferred_element_type=jnp.float32)
+        up_out = lax.dot_general(x, up[...], turned, preferred_element_type=jnp.float32)
         inner = (gate_out / (1.0 + jnp.exp(-gate_out)) * up_out).astype(jnp.bfloat16)
         tile = DOWN_TILE if width % DOWN_TILE == 0 else width
         for at in range(0, width, tile):
@@ -271,28 +285,30 @@
     lax.fori_loop(0, PLANES * stages, step, 0)
     join_cores(PLANES * stages - 1)
 
+    def add_piece(fed, copy, mine, across, along):
+        @pl.when(fed)
+        def _():
+            copy.wait_recv()
+            part[mine, :] = (
+                wide(part, mine) + wide(from_plane, across) + wide(from_stage, along)
+            ).astype(part.dtype)
+
+        @pl.when(jnp.logical_not(fed))
+        def _():
+            part[mine, :] = (wide(part, mine) + wide(from_plane, across)).astype(part.dtype)
+
     def chain(j, carry):
         far = near_first(z, stages - 1 - j, stages)
         down_way = far < z
         slot = jnp.where(down_way, far, far + 1)
         target = index_of(jnp.where(down_way, z - 1, z + 1), y, c)
         fed = jnp.where(down_way, z < stages - 1, z > 0)
-        mine = span(index_of(far, y, c))
         plane_copy(far).wait_recv()
-        copy = stage_copy(far, slot, target)
-
-        @pl.when(fed)
-        def _():
-            copy.wait_recv()
-            part[mine, :] = (
-                wide(part, mine) + wide(from_plane, span(far)) + wide(from_stage, span(slot))
-            ).astype(part.dtype)
-
-        @pl.when(jnp.logical_not(fed))
-        def _():
-            part[mine, :] = (wide(part, mine) + wide(from_plane, span(far))).astype(part.dtype)
-
-        copy.start()
+        for p in range(PIECES):
+            mine = piece(index_of(far, y, c), p)
+            copy = stage_copy(far, slot, target, p)
+            add_piece(fed, copy, mine, piece(far, p), piece(slot, p))
+            copy.start()
         return carry
 
     lax.fori_loop(0, stages - 1, chain, 0)
@@ -303,12 +319,14 @@
 
     @pl.when(z < stages - 1)
     def _():
-        stage_copy(z, z, index_of(z, 1 - y, c)).wait_recv()
+        for p in range(PIECES):
+            stage_copy(z, z, index_of(z, 1 - y, c), p).wait_recv()
         out_ref[...] += wide(from_stage, span(z))
 
     @pl.when(z > 0)
     def _():
-        stage_copy(z, z + 1, index_of(z, 1 - y, c)).wait_recv()
+        for p in range(PIECES):
+            stage_copy(z, z + 1, index_of(z, 1 - y, c), p).wait_recv()
         out_ref[...] += wide(from_stage, span(z + 1))
 
     def settle(i, carry):
@@ -319,7 +337,9 @@
 
     def settle_stage(i, carry):
         plane_copy(i).wait_send()
-        pl.when(i != z)(lambda: stage_copy(i, i, index_of(z, 1 - y, c)).wait_send())
+        for p in range(PIECES):
+            stage = stage_copy(i, i, index_of(z, 1 - y, c), p)
+            pl.when(i != z)(stage.wait_send)
         return carry
 
     lax.fori_loop(0, stages, settle_stage, 0)
@@ -344,14 +364,14 @@
             pltpu.VMEM((n // CORES * rows, width), bf16),
             pltpu.VMEM((stages * rows, width), bf16),
             pltpu.VMEM(((stages + 1) * rows, width), bf16),
-            pltpu.SemaphoreType.DMA((n, 4)),
-            pltpu.SemaphoreType.DMA((n,)),
+            pltpu.SemaphoreType.DMA((n, 4, PIECES)),
+            pltpu.SemaphoreType.DMA((n, PIECES)),
             pltpu.SemaphoreType.DMA((n // CORES,)),
             pltpu.SemaphoreType.DMA((n // CORES,)),
             pltpu.SemaphoreType.DMA((stages,)),
             pltpu.SemaphoreType.DMA((stages,)),
-            pltpu.SemaphoreType.DMA((stages,)),
-            pltpu.SemaphoreType.DMA((stages + 1,)),
+            pltpu.SemaphoreType.DMA((stages, PIECES)),
+            pltpu.SemaphoreType.DMA((stages + 1, PIECES)),
             pltpu.SemaphoreType.DMA((4,)),
         ],
         compiler_params=pltpu.CompilerParams(
@@ -429,7 +449,7 @@
         my_counts, capacity
     )
     target = jnp.where(valid, rows_flat, tok_rows)
-    summed = feed_forward(devices, normed, gate_weight, up_weight, down_weight)
+    summed = feed_forward(devices, normed, gate_weight.T, up_weight.T, down_weight)
     live_mask = jnp.zeros((tok_rows,), jnp.float32).at[target].set(1.0, mode="drop")
     ffn_round = lax.optimization_barrier(summed.astype(jnp.bfloat16))
     ffn_back = ffn_round.astype(jnp.float32) * live_mask[:, None]

time: 183 us -> 172 us (0.940)
  local copies, waits for them, and re-layouts: 12.8 us -> 3.54 us
  Pallas kernels: 154 us -> 151 us
    unnamed x14 -> x10, local copies, waits for them, and re-layouts: 9.44 us -> 0.22 us
    pallas_call x1, Pallas kernels: 133 us -> 131 us  [feed_forward(): pl.pallas_call(functools.partial(ffn_kernel, n), out_shape=jax.ShapeDtype...]
where the time goes in v2:
time: 172 us
  Pallas kernels  151 us (88%)
  other arithmetic  11.2 us (7%)
  matrix products  5.37 us (3%)
  local copies, waits for them, and re-layouts  3.54 us (2%)
    pallas_call x1, Pallas kernels, feed_forward(): pl.pallas_call(functools.partial(ffn_kernel, n), out_shape=jax.ShapeDtype...  131 us
    pallas_call x1, Pallas kernels, gather_rows(): pl.pallas_call(functools.partial(gather_kernel, n), out_shape=jax.ShapeDt...  20.8 us

profile of v2, /device:TPU:0, one launch (start us, length us, event | category | flops | bytes accessed | tf_op | source)
XLA Modules:
  0.0 171.7 jit_solution(8507096718758760015)
XLA Ops:
  0.0 0.0 copy-start
  0.0 0.7 dynamic-slice_bitcast_fusion
  0.7 0.8 dynamic_slice.9
  1.5 0.8 dynamic_slice.10
  2.3 0.1 iota_compare_fusion.1
  2.3 0.1 lt.36
  2.4 0.7 fusion.26
  3.1 1.0 scatter_custom_fusion
  4.1 0.7 broadcast_compare_fusion
  4.8 1.4 pad_maximum_fusion.x_ref
  6.2 3.1 %fusion.12 = pred[128,2048]{0,1:T(8,128)(4,1)S(1)} fusion(s32[128]{0:T(128)S(1)} %dynamic_slice.10, s32[128]{0:T(128)S(1)} %iota_add_fusion, s32[128]{0:T(128)S(1)} %dynamic_slice.9, s32[2048]{0:T(1024)} %param.23, s32[2048]{0:T(1024)} %param.22, pred[2048]{0:T(1024)(128)(4,1)S(1)} %broadcast_compare_fusion), kind=kLoop, calls=%fused_computation.17 | loop fusion | flops 1572864 | bytes 282112 | tf_op jit(solution)/shard_map/and | solution.py:414
  9.3 20.8 %shard_map.127 = bf16[2048,256]{1,0:T(8,128)(2,1)} custom-call(bf16[128,256]{1,0:T(8,128)(2,1)} %pad_maximum_fusion.x_ref), custom_call_target="tpu_custom_call" | custom-call | tf_op jit(solution)/shard_map/pallas_call | solution.py:145
  30.0 0.0 copy-done
  30.0 0.0 copy-start.2
  30.0 2.5 %fusion = (f32[8,128]{1,0:T(8,128)S(1)}, f32[2048,128,8]{1,0,2:T(8,128)S(1)}) fusion(pred[128,2048]{0,1:T(8,128)(4,1)S(1)} %fusion.12, bf16[2048,256]{1,0:T(8,128)(2,1)} %shard_map.127, bf16[128,1024]{1,0:T(8,128)(2,1)S(1)} %copy-done), kind=kOutput, calls=%fused_computation.3 | convolution fusion | flops 543161344 | bytes 9441280 | tf_op jit(solution)/shard_map/tqd,kd->qtk/dot_general | solution.py:420
  32.6 2.0 %fusion.1 = f32[8,128]{1,0:T(8,128)S(1)} fusion(f32[2048,128,8]{1,0,2:T(8,128)S(1)} %get-tuple-element.6, f32[8,128]{1,0:T(8,128)S(1)} %broadcast_maximum_fusion, pred[128,2048]{0,1:T(8,128)(4,1)S(1)} %fusion.12), kind=kLoop, calls=%fused_computation.4 | loop fusion | flops 10484736 | bytes 8658944 | tf_op jit(solution)/shard_map/reduce_sum | solution.py:426
  34.6 0.0 copy-done.2
  34.6 0.0 copy-start.1
  34.6 0.0 copy-start.3
  34.6 0.0 copy-start.4
  34.6 2.1 %fusion.16 = bf16[128,8,128]{0,2,1:T(8,128)(2,1)S(1)} fusion(f32[2048,128,8]{1,0,2:T(8,128)S(1)} %get-tuple-element.6, f32[8,128]{1,0:T(8,128)S(1)} %broadcast_maximum_fusion, pred[128,2048]{0,1:T(8,128)(4,1)S(1)} %fusion.12, bf16[2048,256]{1,0:T(8,128)(2,1)S(1)} %copy-done.2, f32[128,8]{0,1:T(8,128)S(1)} %bitcast.58), kind=kOutput, calls=%fused_computation.19 | convolution fusion | flops 547618816 | bytes 9445376 | tf_op jit(solution)/shard_map/qtk,kd->qtd/dot_general | solution.py:427
  36.7 0.1 copy-done.1
  36.8 0.1 copy-done.3
  36.9 0.8 multiply_reduce_fusion
  37.7 0.0 copy-done.4
  37.7 1.0 multiply_convert_fusion.x_hbm
  38.7 130.7 %shard_map.128 = f32[128,2048]{1,0:T(8,128)} custom-call(bf16[128,2048]{1,0:T(8,128)(2,1)} %multiply_convert_fusion.x_hbm, bf16[688,2048]{1,0:T(8,128)(2,1)} %bitcast.55, bf16[688,2048]{1,0:T(8,128)(2,1)} %bitcast.56, bf16[688,2048]{1,0:T(8,128)(2,1)} %down_hbm.1), custom_call_target="tpu_custom_call" | custom-call | tf_op jit(solution)/shard_map/pallas_call | solution.py:353
  169.4 1.3 convert_element_type.38
  170.7 1.0 add_convert_fusion
  (4 shorter events, 0.0 us)
Async XLA Ops:
  0.0 30.0 %copy-start = (bf16[128,1024]{1,0:T(8,128)(2,1)S(1)}, bf16[128,1024]{1,0:T(8,128)(2,1)}, u32[]{:S(2)}) copy-start(bf16[128,1024]{1,0:T(8,128)(2,1)} %param.14) | copy-start | bytes 786436
  30.0 4.5 %copy-start.2 = (bf16[2048,256]{1,0:T(8,128)(2,1)S(1)}, bf16[2048,256]{1,0:T(8,128)(2,1)}, u32[]{:S(2)}) copy-start(bf16[2048,256]{1,0:T(8,128)(2,1)} %shard_map.127) | copy-start | bytes 3145732
  34.6 2.2 %copy-start.1 = (bf16[1024,2048]{1,0:T(8,128)(2,1)S(1)}, bf16[1024,2048]{1,0:T(8,128)(2,1)}, u32[]{:S(2)}) copy-start(bf16[1024,2048]{1,0:T(8,128)(2,1)} %param.17) | copy-start | bytes 12582916
  34.6 2.3 %copy-start.3 = (bf16[128,2048]{1,0:T(8,128)(2,1)S(1)}, bf16[128,2048]{1,0:T(8,128)(2,1)}, u32[]{:S(2)}) copy-start(bf16[128,2048]{1,0:T(8,128)(2,1)} %param.13) | copy-start | bytes 1572868
  34.6 3.1 %copy-start.4 = (f32[2048]{0:T(1024)S(1)}, f32[2048]{0:T(1024)}, u32[]{:S(2)}) copy-start(f32[2048]{0:T(1024)} %param.18) | copy-start | bytes 24580

commit v3 on v2

--- a/solution.py
+++ b/solution.py
@@ -171,6 +171,7 @@
     from_core,
     from_plane,
     from_stage,
+    from_other,
     send,
     recv,
     core_send,
@@ -216,27 +217,33 @@
             index_of(z, y, 1 - c),
         )
 
-    def plane_copy(far):
+    piece_rows = rows // PIECES
+
+    def piece(b, p):
+        return pl.ds(pl.multiple_of(b * rows + p * piece_rows, piece_rows), piece_rows)
+
+    def plane_copy(far, p=0):
+        slot = far if p == 0 else stages
         return remote(
-            part.at[span(index_of(far, 1 - y, c))],
-            from_plane.at[span(far)],
-            plane_send.at[far],
-            plane_recv.at[far],
+            part.at[piece(index_of(far, 1 - y, c), p)],
+            from_plane.at[piece(far, p)],
+            plane_send.at[slot],
+            plane_recv.at[slot],
             index_of(z, 1 - y, c),
         )
 
-    piece_rows = rows // PIECES
-
-    def piece(b, p):
-        return pl.ds(pl.multiple_of(b * rows + p * piece_rows, piece_rows), piece_rows)
-
-    def stage_copy(far, slot, target, p):
+    def sent(far, q):
+        return piece(index_of(far, 1 - y if q == 2 else y, c), min(q, 1))
+
+    def landed(slot, q):
+        if q == 2:
+            return from_other, pl.ds(pl.multiple_of(slot * piece_rows, piece_rows), piece_rows)
+        return from_stage, piece(slot, q)
+
+    def stage_copy(far, slot, target, q):
+        ref, where = landed(slot, q)
         return remote(
-            part.at[piece(index_of(far, y, c), p)],
-            from_stage.at[piece(slot, p)],
-            stage_send.at[far, p],
-            stage_recv.at[slot, p],
-            target,
+            part.at[sent(far, q)], ref.at[where], stage_send.at[far, q], stage_recv.at[slot, q], target
         )
 
     def wide(ref, where):
@@ -285,17 +292,19 @@
     lax.fori_loop(0, PLANES * stages, step, 0)
     join_cores(PLANES * stages - 1)
 
-    def add_piece(fed, copy, mine, across, along):
+    def add(mine, ref, where):
+        part[mine, :] = (wide(part, mine) + wide(ref, where)).astype(part.dtype)
+
+    def add_piece(fed, copy, far, slot, q):
+        mine = sent(far, q)
+        if q == 0:
+            plane_copy(far).wait_recv()
+            add(mine, from_plane, piece(far, 0))
+
         @pl.when(fed)
         def _():
             copy.wait_recv()
-            part[mine, :] = (
-                wide(part, mine) + wide(from_plane, across) + wide(from_stage, along)
-            ).astype(part.dtype)
-
-        @pl.when(jnp.logical_not(fed))
-        def _():
-            part[mine, :] = (wide(part, mine) + wide(from_plane, across)).astype(part.dtype)
+            add(mine, *landed(slot, q))
 
     def chain(j, carry):
         far = near_first(z, stages - 1 - j, stages)
@@ -303,17 +312,19 @@
         slot = jnp.where(down_way, far, far + 1)
         target = index_of(jnp.where(down_way, z - 1, z + 1), y, c)
         fed = jnp.where(down_way, z < stages - 1, z > 0)
-        plane_copy(far).wait_recv()
-        for p in range(PIECES):
-            mine = piece(index_of(far, y, c), p)
-            copy = stage_copy(far, slot, target, p)
-            add_piece(fed, copy, mine, piece(far, p), piece(slot, p))
+        for q in (2, 1, 0):
+            copy = stage_copy(far, slot, target, q)
+            add_piece(fed, copy, far, slot, q)
             copy.start()
         return carry
 
     lax.fori_loop(0, stages - 1, chain, 0)
 
+    for slot, there in ((z, z < stages - 1), (z + 1, z > 0)):
+        add_piece(there, stage_copy(z, slot, index_of(z, 1 - y, c), 2), z, slot, 2)
+    plane_copy(z, 1).start()
     plane_copy(z).wait_recv()
+    plane_copy(z, 1).wait_recv()
     mine = span(me)
     out_ref[...] = wide(part, mine) + wide(from_plane, span(z))
 
@@ -337,12 +348,13 @@
 
     def settle_stage(i, carry):
         plane_copy(i).wait_send()
-        for p in range(PIECES):
-            stage = stage_copy(i, i, index_of(z, 1 - y, c), p)
+        for q in range(3):
+            stage = stage_copy(i, i, index_of(z, 1 - y, c), q)
             pl.when(i != z)(stage.wait_send)
         return carry
 
     lax.fori_loop(0, stages, settle_stage, 0)
+    plane_copy(z, 1).wait_send()
     spread.finish()
 
 
@@ -364,14 +376,15 @@
             pltpu.VMEM((n // CORES * rows, width), bf16),
             pltpu.VMEM((stages * rows, width), bf16),
             pltpu.VMEM(((stages + 1) * rows, width), bf16),
+            pltpu.VMEM(((stages + 1) * (rows // PIECES), width), bf16),
             pltpu.SemaphoreType.DMA((n, 4, PIECES)),
             pltpu.SemaphoreType.DMA((n, PIECES)),
             pltpu.SemaphoreType.DMA((n // CORES,)),
             pltpu.SemaphoreType.DMA((n // CORES,)),
-            pltpu.SemaphoreType.DMA((stages,)),
-            pltpu.SemaphoreType.DMA((stages,)),
-            pltpu.SemaphoreType.DMA((stages, PIECES)),
-            pltpu.SemaphoreType.DMA((stages + 1, PIECES)),
+            pltpu.SemaphoreType.DMA((stages + 1,)),
+            pltpu.SemaphoreType.DMA((stages + 1,)),
+            pltpu.SemaphoreType.DMA((stages, 3)),
+            pltpu.SemaphoreType.DMA((stages + 1, 3)),
             pltpu.SemaphoreType.DMA((4,)),
         ],
         compiler_params=pltpu.CompilerParams(

time: 172 us -> 163 us (0.948); the launches traced: 172 us -> 161 us
  Pallas kernels: 151 us -> 140 us
    pallas_call x1, Pallas kernels: 131 us -> 120 us  [feed_forward(): pl.pallas_call(functools.partial(ffn_kernel, n), out_shape=jax.ShapeDtype...]
where the time goes in v3:
time: 163 us; the launch traced here: 161 us
  Pallas kernels  140 us (86%)
  other arithmetic  11.2 us (7%)
  matrix products  5.37 us (3%)
  local copies, waits for them, and re-layouts  3.54 us (2%)
    pallas_call x1, Pallas kernels, feed_forward(): pl.pallas_call(functools.partial(ffn_kernel, n), out_shape=jax.ShapeDtype...  120 us
    pallas_call x1, Pallas kernels, gather_rows(): pl.pallas_call(functools.partial(gather_kernel, n), out_shape=jax.ShapeDt...  20.8 us

profile of v3, /device:TPU:0, one launch (start us, length us, event | category | flops | bytes accessed | tf_op | source)
XLA Modules:
  0.0 160.6 jit_solution(4521364264808240600)
XLA Ops:
  0.0 0.0 copy-start
  0.0 0.7 dynamic-slice_bitcast_fusion
  0.7 0.8 dynamic_slice.9
  1.5 0.8 dynamic_slice.10
  2.3 0.1 iota_compare_fusion.1
  2.3 0.1 lt.36
  2.4 0.7 fusion.26
  3.1 1.0 scatter_custom_fusion
  4.1 0.7 broadcast_compare_fusion
  4.8 1.4 pad_maximum_fusion.x_ref
  6.2 3.1 %fusion.12 = pred[128,2048]{0,1:T(8,128)(4,1)S(1)} fusion(s32[128]{0:T(128)S(1)} %dynamic_slice.10, s32[128]{0:T(128)S(1)} %iota_add_fusion, s32[128]{0:T(128)S(1)} %dynamic_slice.9, s32[2048]{0:T(1024)} %param.23, s32[2048]{0:T(1024)} %param.22, pred[2048]{0:T(1024)(128)(4,1)S(1)} %broadcast_compare_fusion), kind=kLoop, calls=%fused_computation.17 | loop fusion | flops 1572864 | bytes 282112 | tf_op jit(solution)/shard_map/and | solution.py:427
  9.3 20.8 %shard_map.127 = bf16[2048,256]{1,0:T(8,128)(2,1)} custom-call(bf16[128,256]{1,0:T(8,128)(2,1)} %pad_maximum_fusion.x_ref), custom_call_target="tpu_custom_call" | custom-call | tf_op jit(solution)/shard_map/pallas_call | solution.py:145
  30.0 0.0 copy-done
  30.0 0.0 copy-start.2
  30.0 2.5 %fusion = (f32[8,128]{1,0:T(8,128)S(1)}, f32[2048,128,8]{1,0,2:T(8,128)S(1)}) fusion(pred[128,2048]{0,1:T(8,128)(4,1)S(1)} %fusion.12, bf16[2048,256]{1,0:T(8,128)(2,1)} %shard_map.127, bf16[128,1024]{1,0:T(8,128)(2,1)S(1)} %copy-done), kind=kOutput, calls=%fused_computation.3 | convolution fusion | flops 543161344 | bytes 9441280 | tf_op jit(solution)/shard_map/tqd,kd->qtk/dot_general | solution.py:433
  32.6 2.0 %fusion.1 = f32[8,128]{1,0:T(8,128)S(1)} fusion(f32[2048,128,8]{1,0,2:T(8,128)S(1)} %get-tuple-element.6, f32[8,128]{1,0:T(8,128)S(1)} %broadcast_maximum_fusion, pred[128,2048]{0,1:T(8,128)(4,1)S(1)} %fusion.12), kind=kLoop, calls=%fused_computation.4 | loop fusion | flops 10484736 | bytes 8658944 | tf_op jit(solution)/shard_map/reduce_sum | solution.py:439
  34.6 0.0 copy-done.2
  34.6 0.0 copy-start.1
  34.6 0.0 copy-start.3
  34.6 0.0 copy-start.4
  34.6 2.1 %fusion.16 = bf16[128,8,128]{0,2,1:T(8,128)(2,1)S(1)} fusion(f32[2048,128,8]{1,0,2:T(8,128)S(1)} %get-tuple-element.6, f32[8,128]{1,0:T(8,128)S(1)} %broadcast_maximum_fusion, pred[128,2048]{0,1:T(8,128)(4,1)S(1)} %fusion.12, bf16[2048,256]{1,0:T(8,128)(2,1)S(1)} %copy-done.2, f32[128,8]{0,1:T(8,128)S(1)} %bitcast.58), kind=kOutput, calls=%fused_computation.19 | convolution fusion | flops 547618816 | bytes 9445376 | tf_op jit(solution)/shard_map/qtk,kd->qtd/dot_general | solution.py:440
  36.7 0.1 copy-done.1
  36.8 0.1 copy-done.3
  36.9 0.8 multiply_reduce_fusion
  37.7 0.0 copy-done.4
  37.7 1.0 multiply_convert_fusion.x_hbm
  38.7 119.6 %shard_map.128 = f32[128,2048]{1,0:T(8,128)} custom-call(bf16[128,2048]{1,0:T(8,128)(2,1)} %multiply_convert_fusion.x_hbm, bf16[688,2048]{1,0:T(8,128)(2,1)} %bitcast.55, bf16[688,2048]{1,0:T(8,128)(2,1)} %bitcast.56, bf16[688,2048]{1,0:T(8,128)(2,1)} %down_hbm.1), custom_call_target="tpu_custom_call" | custom-call | tf_op jit(solution)/shard_map/pallas_call | solution.py:365
  158.3 1.3 convert_element_type.38
  159.6 1.0 add_convert_fusion
  (4 shorter events, 0.0 us)
Async XLA Ops:
  0.0 30.0 %copy-start = (bf16[128,1024]{1,0:T(8,128)(2,1)S(1)}, bf16[128,1024]{1,0:T(8,128)(2,1)}, u32[]{:S(2)}) copy-start(bf16[128,1024]{1,0:T(8,128)(2,1)} %param.14) | copy-start | bytes 786436
  30.0 4.5 %copy-start.2 = (bf16[2048,256]{1,0:T(8,128)(2,1)S(1)}, bf16[2048,256]{1,0:T(8,128)(2,1)}, u32[]{:S(2)}) copy-start(bf16[2048,256]{1,0:T(8,128)(2,1)} %shard_map.127) | copy-start | bytes 3145732
  34.6 2.2 %copy-start.1 = (bf16[1024,2048]{1,0:T(8,128)(2,1)S(1)}, bf16[1024,2048]{1,0:T(8,128)(2,1)}, u32[]{:S(2)}) copy-start(bf16[1024,2048]{1,0:T(8,128)(2,1)} %param.17) | copy-start | bytes 12582916
  34.6 2.3 %copy-start.3 = (bf16[128,2048]{1,0:T(8,128)(2,1)S(1)}, bf16[128,2048]{1,0:T(8,128)(2,1)}, u32[]{:S(2)}) copy-start(bf16[128,2048]{1,0:T(8,128)(2,1)} %param.13) | copy-start | bytes 1572868
  34.6 3.1 %copy-start.4 = (f32[2048]{0:T(1024)S(1)}, f32[2048]{0:T(1024)}, u32[]{:S(2)}) copy-start(f32[2048]{0:T(1024)} %param.18) | copy-start | bytes 24580
